TPU v7x, 512 devices: a whole 4x4x16 slice. The times are simulated.
512 devices in a mesh: blk: 64 (over z_hi, y, x, core), grp: 8 (over z_lo).
Axes of the slice: x: 4, y: 4, z: 16 (z_hi: 2, z_lo: 8; z = z_hi * 8 + z_lo), core: 2. Of those that a mesh axis runs over, the one named last changes fastest.
Arguments:
- samples: float32 [32, 16384], P(None, ('blk', 'grp')), may hold values from 0 to 256
- bounds: int32 [2, 32, 8192], P(None, None, 'blk'), may hold values from 0 to 256, as said below
- spread: float32 [32], replicated, may hold values from 2 to 8
- counts: int32 [8192], P('blk'), may hold values from 0 to 2047
Outputs:
- log_estimate: float32 [8192], P('blk')
- spread_grad: float32 [32], replicated
Inputs may be any that keep to these rules, and one draw needn't show every extreme that they name: For every query and dimension bounds[0] < bounds[1]; each query restricts exactly 3 dimensions to a width of 16 to 48 cells and has bounds 0 and 256 in all others.
All inputs are finite; a program needn't handle non-finite values.
Results may differ from a plain program's by a relative error of at most 0.0003.
Values sent between devices are 32-bit elements; how exact they have to be, the bound alone decides.
A program may use at most 64 MiB of HBM per device.

v0:
```python
import math
import jax
import jax.numpy as jnp
from jax import lax
from jax.sharding import PartitionSpec as P

TABLE_ROWS = 1048576
root_half = 0.7071067811865476
density_norm = 0.3989422804014327


def box_terms(lower_edge, upper_edge, points, inverse):
    upper_arg = (upper_edge - points) * inverse
    lower_arg = (lower_edge - points) * inverse
    in_box = 0.5 * (lax.erf(upper_arg * root_half) - lax.erf(lower_arg * root_half))
    slopes = density_norm * (
        lower_arg * jnp.exp(-0.5 * lower_arg * lower_arg)
        - upper_arg * jnp.exp(-0.5 * upper_arg * upper_arg)
    )
    prefix_prod = jnp.cumprod(in_box, axis=0)
    behind = jnp.flip(jnp.cumprod(jnp.flip(in_box, 0), axis=0), 0)
    unit_row = jnp.ones_like(in_box[:1])
    before = jnp.concatenate([unit_row, prefix_prod[:-1]], 0)
    after_dims = jnp.concatenate([behind[1:], unit_row], 0)
    return (prefix_prod[-1], before * after_dims * slopes)


def finish(est_sum, counts_float, sample_total, query_total):
    smoothing = 1.0 / TABLE_ROWS
    estimate = est_sum / sample_total
    log_est = jnp.log(estimate + smoothing)
    target = jnp.log(counts_float / TABLE_ROWS + smoothing)
    weight = 2.0 * (log_est - target) / (query_total * (estimate + smoothing))
    return (log_est, weight)


def on_device(samples, bounds, spread, counts):
    inverse = 1.0 / spread
    lower_edge = bounds[0].astype(jnp.float32)
    upper_edge = bounds[1].astype(jnp.float32)
    dims = samples.shape[0]
    local_queries = bounds.shape[2]
    sample_total = samples.shape[1] * lax.axis_size("blk") * lax.axis_size("grp")
    query_total = local_queries * lax.axis_size("blk")
    initial = (
        jnp.zeros((local_queries,), jnp.float32),
        jnp.zeros((dims, local_queries), jnp.float32),
    )
    piece = lax.all_gather(samples, "blk", axis=1, tiled=True)
    row_count = piece.shape[1]
    width_rows = math.gcd(row_count, 32)
    blocks = piece.reshape(dims, row_count // width_rows, width_rows).transpose(1, 0, 2)

    def advance(inner, points):
        totals, gradients = box_terms(
            lower_edge[:, :, None],
            upper_edge[:, :, None],
            points[:, None, :],
            inverse[:, None, None],
        )
        return ((inner[0] + totals.sum(axis=1), inner[1] + gradients.sum(axis=2)), None)

    est_sum, grad_sum = lax.scan(advance, initial, blocks)[0]
    est_sum, grad_sum = lax.psum((est_sum, grad_sum), "grp")
    log_est, weight = finish(est_sum, counts.astype(jnp.float32), sample_total, query_total)
    share = jnp.dot(grad_sum, weight, precision=lax.Precision.HIGHEST) / sample_total
    gradient = lax.psum(share, "blk")
    return (log_est, gradient)


def solution(mesh):
    return jax.shard_map(
        on_device,
        mesh=mesh,
        in_specs=(P(None, ("blk", "grp")), P(None, None, "blk"), P(), P("blk")),
        out_specs=(P("blk"), P()),
        check_vma=False,
    )
```

profile of v0, /device:TPU:1, one launch (start us, length us, event | category | flops | bytes accessed | tf_op | source)
XLA Modules:
  0.0 701.9 jit_solution(682669079754419878)
XLA Ops:
  2.1 168.5 %all_gather.3 = f32[32,2048]{0,1:T(8,128)S(1)} all-gather(f32[32,32]{0,1:T(8,128)S(1)} %copy.7), channel_id=1, replica_groups=mesh['blk'=64,'grp'=8] {'blk'}, dimensions={1}, use_global_device_ids=true | all-gather | bytes 266240 | tf_op jit(solution)/shard_map/all_gather | solution.py:49
  170.6 199.7 %while.13 = (s32[]{:T(128)}, f32[128]{0:T(128)S(1)}, f32[32,128]{1,0:T(8,128)S(1)}, f32[32,128]{1,0:T(8,128)S(1)}, f32[64,32,32]{1,2,0:T(8,128)S(1)}, /*index=5*...) while((s32[]{:T(128)}, f32[128]{0:T(128)S(1)}, f32[32,128]{1,0:T(8,128)S(1)}, ...), condition=%wide.region_5.6_spmd.clone, body=%wide.region_0.5_spmd.clone.sunk | while | flops 12198019 | bytes 10025512 | solution.py:63
  172.2 1.0 slice-done
  175.4 1.0 slice-done
  178.5 1.0 slice-done
  181.6 1.0 slice-done
  184.7 1.0 slice-done
  187.9 1.0 slice-done
  191.0 1.0 slice-done
  194.1 1.0 slice-done
  197.2 1.0 slice-done
  200.3 1.0 slice-done
  203.5 1.0 slice-done
  206.6 1.0 slice-done
  209.7 1.0 slice-done
  212.8 1.0 slice-done
  215.9 1.0 slice-done
  219.1 1.0 slice-done
  222.2 1.0 slice-done
  225.3 1.0 slice-done
  228.4 1.0 slice-done
  231.5 1.0 slice-done
  237.8 1.0 slice-done
  240.9 1.0 slice-done
  247.1 1.0 slice-done
  250.3 1.0 slice-done
  259.6 1.0 slice-done
  269.0 1.0 slice-done
  278.3 1.0 slice-done
  281.5 1.0 slice-done
  287.7 1.0 slice-done
  290.8 1.0 slice-done
  297.1 1.0 slice-done
  300.2 1.0 slice-done
  306.4 1.0 slice-done
  309.6 1.0 slice-done
  318.9 1.0 slice-done
  328.3 1.0 slice-done
  337.6 1.0 slice-done
  340.8 1.0 slice-done
  347.0 1.0 slice-done
  350.1 1.0 slice-done
  356.4 1.0 slice-done
  359.5 1.0 slice-done
  365.7 1.0 slice-done
  368.8 1.0 slice-done
  370.3 45.3 %all-reduce.2 = (f32[128]{0:T(128)S(1)}, f32[32,128]{1,0:T(8,128)S(1)}) all-reduce(f32[128]{0:T(128)S(1)} %get-tuple-element.40, f32[32,128]{1,0:T(8,128)S(1)} %get-tuple-element.41), channel_id=1, replica_groups=mesh['blk'=64,'grp'=8] {'grp'}, use_global_device_ids=true, to_apply=%region_6.7 | all-reduce | flops 4224 | bytes 33792 | tf_op jit(solution)/shard_map/psum | solution.py:64
  416.7 285.1 %psum.23 = f32[32]{0:T(128)} all-reduce(f32[32]{0:T(128)S(1)} %fusion.18), channel_id=1, replica_groups=mesh['blk'=64,'grp'=8] {'blk'}, use_global_device_ids=true, to_apply=%region_8.9 | all-reduce | flops 32 | bytes 256 | tf_op jit(solution)/shard_map/psum | solution.py:67
  (995 shorter events, 152.7 us)
Async XLA Ops:
  0.6 1.4 copy-start.1
  172.2 1.0 slice-start
  175.3 1.0 slice-start
  178.4 1.0 slice-start
  181.6 1.0 slice-start
  184.7 1.0 slice-start
  187.8 1.0 slice-start
  190.9 1.0 slice-start
  194.0 1.0 slice-start
  197.2 1.0 slice-start
  200.3 1.0 slice-start
  203.4 1.0 slice-start
  206.5 1.0 slice-start
  209.6 1.0 slice-start
  212.8 1.0 slice-start
  215.9 1.0 slice-start
  219.0 1.0 slice-start
  222.1 1.0 slice-start
  225.2 1.0 slice-start
  228.4 1.0 slice-start
  231.5 1.0 slice-start
  234.6 1.0 slice-start
  237.7 1.0 slice-start
  240.8 1.0 slice-start
  244.0 1.0 slice-start
  247.1 1.0 slice-start
  250.2 1.0 slice-start
  253.3 1.0 slice-start
  256.4 1.0 slice-start
  259.6 1.0 slice-start
  262.7 1.0 slice-start
  265.8 1.0 slice-start
  268.9 1.0 slice-start
  272.1 1.0 slice-start
  278.3 1.0 slice-start
  287.7 1.0 slice-start
  297.0 1.0 slice-start
  300.1 1.0 slice-start
  306.4 1.0 slice-start
  309.5 1.0 slice-start
  318.9 1.0 slice-start
  328.2 1.0 slice-start
  337.6 1.0 slice-start
  346.9 1.0 slice-start
  356.3 1.0 slice-start
  359.4 1.0 slice-start
  365.7 1.0 slice-start
  368.8 1.0 slice-start
  (84 other events, 70.0 us)
where the time goes:
time: 705 us; the launch traced here: 702 us
  blocking collectives  499 us (71%)
  local copies, waits for them, and re-layouts  126 us (18%)
  other arithmetic  69.8 us (10%)
    psum x1, blocking collectives, on_device(): gradient = lax.psum(share, 'blk')  285 us
    all_gather x1, blocking collectives, on_device(): piece = lax.all_gather(samples, 'blk', axis=1, tiled=True)  169 us
    slice x128, local copies, waits for them, and re-layouts, box_terms(): before = jnp.concatenate([unit_row, prefix_prod[:-1]], 0)  63.2 us
    while x128, local copies, waits for them, and re-layouts  48.7 us
    psum x1, blocking collectives, on_device(): est_sum, grad_sum = lax.psum((est_sum, grad_sum), 'grp')  45.3 us
    reduce_sum x64, other arithmetic, advance(): gradients.sum(axis=2)  28.5 us
    another operation x64, other arithmetic, box_terms(): prefix_prod = jnp.cumprod(in_box, axis=0)  18.5 us
    sub x64, other arithmetic, box_terms(): lax.erf(upper_arg * root_half) - lax.erf(lower_arg * root_half)  17.2 us

commit v1 on v0

--- a/solution.py
+++ b/solution.py
@@ -46,7 +46,9 @@
         jnp.zeros((local_queries,), jnp.float32),
         jnp.zeros((dims, local_queries), jnp.float32),
     )
-    piece = lax.all_gather(samples, "blk", axis=1, tiled=True)
+    piece = jnp.concatenate(
+        lax.all_to_all(jnp.stack([samples] * lax.axis_size("blk")), "blk", 0, 0), axis=1
+    )
     row_count = piece.shape[1]
     width_rows = math.gcd(row_count, 32)
     blocks = piece.reshape(dims, row_count // width_rows, width_rows).transpose(1, 0, 2)

time: 705 us -> 581 us (0.82)
  blocking collectives: 499 us -> 336 us
  starting transfers between devices: 0 us -> 22.4 us
  waiting for transfers between devices: 0 us -> 18 us
    all_gather x1 -> x0, blocking collectives: 169 us -> none  [on_device(): piece = lax.all_gather(samples, 'blk', axis=1, tiled=True)]
    all_to_all x0 -> x1, starting transfers between devices: none -> 22.4 us  [on_device(): lax.all_to_all(jnp.stack([samples] * lax.axis_size('blk')), 'blk', 0, 0)]
    all_to_all x0 -> x1, waiting for transfers between devices: none -> 18 us  [on_device(): lax.all_to_all(jnp.stack([samples] * lax.axis_size('blk')), 'blk', 0, 0)]
  transfers between devices with their start and end apart: 0 -> 1, of which waited for: 0 -> 1; matrix products, arithmetic and copies ran while one was open for 0% -> 0% of each run, Pallas kernels for 0% -> 0%
where the time goes in v1:
time: 581 us; the launch traced here: 578 us
  blocking collectives  336 us (58%)
  local copies, waits for them, and re-layouts  123 us (21%)
  other arithmetic  70.9 us (12%)
  starting transfers between devices  22.4 us (4%)
  waiting for transfers between devices  18 us (3%)
  loops' own time  6.23 us (1%)
    psum x1, blocking collectives, on_device(): gradient = lax.psum(share, 'blk')  285 us
    slice x128, local copies, waits for them, and re-layouts, box_terms(): before = jnp.concatenate([unit_row, prefix_prod[:-1]], 0)  63.2 us
    psum x1, blocking collectives, on_device(): est_sum, grad_sum = lax.psum((est_sum, grad_sum), 'grp')  50.6 us
    while x128, local copies, waits for them, and re-layouts  48.7 us
    reduce_sum x64, other arithmetic, advance(): gradients.sum(axis=2)  28.5 us
    all_to_all x1, starting transfers between devices, on_device(): lax.all_to_all(jnp.stack([samples] * lax.axis_size('blk')), 'blk', 0, 0)  22.4 us
    another operation x64, other arithmetic, box_terms(): prefix_prod = jnp.cumprod(in_box, axis=0)  18.3 us
    all_to_all x1, waiting for transfers between devices, on_device(): lax.all_to_all(jnp.stack([samples] * lax.axis_size('blk')), 'blk', 0, 0)  18 us
  transfers between devices with their start and end apart: 1, of which 1 were waited for; matrix products, arithmetic and copies ran while one was open for 0% of the time, Pallas kernels for 0%

profile of v1, /device:TPU:1, one launch (start us, length us, event | category | flops | bytes accessed | tf_op | source)
XLA Modules:
  0.0 577.7 jit_solution(5122293165772495759)
XLA Ops:
  1.5 1.1 reshape.15
  2.6 22.4 %all-to-all-start = ((f32[64,1,1024]{2,1,0:T(1,128)}), f32[64,1,1024]{2,1,0:T(1,128)S(1)}, u32[]{:S(2)}, u32[]{:S(2)}) async-start(f32[64,1,1024]{2,1,0:T(1,128)} %reshape.15), calls=%async_computation | async-start | bytes 524288 | tf_op jit(solution)/shard_map/all_to_all | solution.py:50
  25.7 18.0 %all-to-all-done = f32[64,1,1024]{2,1,0:T(1,128)S(1)} async-done(((f32[64,1,1024]{2,1,0:T(1,128)}), f32[64,1,1024]{2,1,0:T(1,128)S(1)}, u32[]{:S(2)}, u32[]{:S(2)}) %all-to-all-start) | async-done | bytes 262176 | tf_op jit(solution)/shard_map/all_to_all | solution.py:50
  44.2 1.3 reduce.1
  45.8 195.1 %while.13 = (s32[]{:T(128)}, f32[128]{0:T(128)S(1)}, f32[32,128]{1,0:T(8,128)S(1)}, f32[32,128]{1,0:T(8,128)S(1)}, f32[64,32,32]{2,1,0:T(8,128)S(1)}, /*index=5*...) while((s32[]{:T(128)}, f32[128]{0:T(128)S(1)}, f32[32,128]{1,0:T(8,128)S(1)}, ...), condition=%wide.region_5.6_spmd.clone, body=%wide.region_0.5_spmd.clone.sunk | while | flops 12198019 | bytes 10017320 | solution.py:65
  47.4 1.0 slice-done
  50.4 1.0 slice-done
  53.5 1.0 slice-done
  56.5 1.0 slice-done
  59.6 1.0 slice-done
  62.6 1.0 slice-done
  65.7 1.0 slice-done
  68.7 1.0 slice-done
  71.8 1.0 slice-done
  74.8 1.0 slice-done
  77.9 1.0 slice-done
  80.9 1.0 slice-done
  84.0 1.0 slice-done
  87.0 1.0 slice-done
  90.1 1.0 slice-done
  93.1 1.0 slice-done
  96.2 1.0 slice-done
  99.2 1.0 slice-done
  102.3 1.0 slice-done
  105.3 1.0 slice-done
  108.4 1.0 slice-done
  132.8 1.0 slice-done
  135.8 1.0 slice-done
  138.8 1.0 slice-done
  141.9 1.0 slice-done
  144.9 1.0 slice-done
  148.0 1.0 slice-done
  151.0 1.0 slice-done
  154.1 1.0 slice-done
  157.1 1.0 slice-done
  160.2 1.0 slice-done
  190.7 1.0 slice-done
  193.7 1.0 slice-done
  196.8 1.0 slice-done
  199.8 1.0 slice-done
  202.9 1.0 slice-done
  205.9 1.0 slice-done
  209.0 1.0 slice-done
  212.0 1.0 slice-done
  215.1 1.0 slice-done
  218.1 1.0 slice-done
  240.9 50.6 %all-reduce.2 = (f32[128]{0:T(128)S(1)}, f32[32,128]{1,0:T(8,128)S(1)}) all-reduce(f32[128]{0:T(128)S(1)} %get-tuple-element.40, f32[32,128]{1,0:T(8,128)S(1)} %get-tuple-element.41), channel_id=1, replica_groups=mesh['blk'=64,'grp'=8] {'grp'}, use_global_device_ids=true, to_apply=%region_6.7 | all-reduce | flops 4224 | bytes 33792 | tf_op jit(solution)/shard_map/psum | solution.py:66
  292.3 285.4 %psum.23 = f32[32]{0:T(128)} all-reduce(f32[32]{0:T(128)S(1)} %fusion.18), channel_id=1, replica_groups=mesh['blk'=64,'grp'=8] {'blk'}, use_global_device_ids=true, to_apply=%region_8.9 | all-reduce | flops 32 | bytes 256 | tf_op jit(solution)/shard_map/psum | solution.py:69
  (936 shorter events, 151.7 us)
Async XLA Ops:
  2.6 23.1 %copy-start.1 = (s32[2,32,128]{2,1,0:T(8,128)S(1)}, s32[2,32,128]{2,1,0:T(8,128)}, u32[]{:S(2)}) copy-start(s32[2,32,128]{2,1,0:T(8,128)} %param.7) | copy-start | bytes 98308
  2.6 41.1 %all-to-all-start = ((f32[64,1,1024]{2,1,0:T(1,128)}), f32[64,1,1024]{2,1,0:T(1,128)S(1)}, u32[]{:S(2)}, u32[]{:S(2)}) async-start(f32[64,1,1024]{2,1,0:T(1,128)} %reshape.15), calls=%async_computation | async-start | bytes 524288 | tf_op jit(solution)/shard_map/all_to_all | solution.py:50
  47.3 1.0 slice-start
  50.4 1.0 slice-start
  53.4 1.0 slice-start
  56.5 1.0 slice-start
  59.5 1.0 slice-start
  62.6 1.0 slice-start
  65.6 1.0 slice-start
  68.7 1.0 slice-start
  71.7 1.0 slice-start
  74.8 1.0 slice-start
  77.8 1.0 slice-start
  80.9 1.0 slice-start
  83.9 1.0 slice-start
  87.0 1.0 slice-start
  90.0 1.0 slice-start
  93.1 1.0 slice-start
  96.1 1.0 slice-start
  99.2 1.0 slice-start
  102.2 1.0 slice-start
  105.3 1.0 slice-start
  108.3 1.0 slice-start
  111.4 1.0 slice-start
  114.4 1.0 slice-start
  117.5 1.0 slice-start
  120.5 1.0 slice-start
  123.6 1.0 slice-start
  126.6 1.0 slice-start
  129.6 1.0 slice-start
  132.7 1.0 slice-start
  135.7 1.0 slice-start
  138.8 1.0 slice-start
  141.8 1.0 slice-start
  144.9 1.0 slice-start
  147.9 1.0 slice-start
  151.0 1.0 slice-start
  154.0 1.0 slice-start
  157.1 1.0 slice-start
  160.1 1.0 slice-start
  190.6 1.0 slice-start
  193.7 1.0 slice-start
  196.7 1.0 slice-start
  199.8 1.0 slice-start
  202.8 1.0 slice-start
  205.9 1.0 slice-start
  208.9 1.0 slice-start
  212.0 1.0 slice-start
  (85 other events, 71.0 us)
